TPU v7x, 32 devices: a whole 2x2x4 slice. The times are simulated.
32 devices in a mesh: ctx: 2 (over y), exp: 16 (over z, x, core).
Axes of the slice: x: 2, y: 2, z: 4, core: 2. Of those that a mesh axis runs over, the one named last changes fastest.
Arguments:
- residual: bfloat16 [16, 128, 2048], P('exp', 'ctx'), may hold values from -1 to 1
- queries: bfloat16 [16, 128, 2048], P('exp', 'ctx'), may hold values from -6 to 6
- key_rows: bfloat16 [16, 128, 256], P('exp', 'ctx'), may hold values from -6 to 6
- value_rows: bfloat16 [16, 128, 256], P('exp', 'ctx'), may hold values from -0.8984375 to 0.8984375
- span_order: int32 [4], replicated, may hold values from 0 to 3, as said below
- norm_gain: float32 [2048], replicated, may hold values from 0.1 to 1.9
- gate_logits: float32 [16, 128, 8], P('exp', 'ctx'), may hold values from -6 to 6
- expert_ids: int32 [16, 128, 8], P('exp', 'ctx'), may hold values from 0 to 15, all different within a row; in each aligned block of 64 rows (0 to 63, 64 to 127, ..., all dimensions but the last counted through in order) at most 32 rows name the same one
- gate_up: bfloat16 [16, 2048, 768], P('exp'), may hold values from -1 to 1
- down_weight: bfloat16 [16, 384, 2048], P('exp'), may hold values from -0.3125 to 0.3125
Outputs:
- layer_out: bfloat16 [16, 128, 2048], P('exp', 'ctx')
Inputs may be any that keep to these rules, and one draw needn't show every extreme that they name: A permutation of 0 to 3; rows b * 32 to b * 32 + 31 of every sequence hold positions span_order[b] * 32 onward. `expert_ids`: each token names 8 different experts; within the 64 rows of one device (aligned blocks of rows) no expert is named by more than 32 tokens.
All inputs are finite; a program needn't handle non-finite values.
Results may differ from a plain program's by a relative error of at most 0.0062.
Values may be sent and summed in bfloat16 or wider, within the bound.
A program may use at most 64 MiB of HBM per device.

v0:
```python
import math
import jax
import jax.numpy as jnp
from jax import lax
from jax.sharding import PartitionSpec as P

KVH = 2
HD = 128
GROUP = 8
HALF = 32
big_negative = -1e30
norm_eps = 1e-06


def span_positions(span_order, first_row, row_total):
    row_index = first_row + jnp.arange(row_total, dtype=jnp.int32)
    onehot = (row_index // HALF)[:, None] == jnp.arange(span_order.shape[0], dtype=jnp.int32)[
        None, :
    ]
    block_start = jnp.sum(jnp.where(onehot, span_order[None, :], 0), axis=1)
    return block_start * HALF + row_index % HALF


def attend_update(state_in, pieces, first_index, query_heads, query_pos, span_order):
    running_max, running_sum, running_out = state_in
    key_piece, value_piece = pieces
    key_count = key_piece.shape[1]
    key_heads = key_piece[0].reshape(key_count, KVH, HD)
    value_heads = value_piece[0].reshape(key_count, KVH, HD)
    key_pos = span_positions(span_order, first_index, key_count)
    score_scale = 1.0 / math.sqrt(HD)
    scores = (
        jnp.einsum("tgqd,cgd->gqtc", query_heads, key_heads, preferred_element_type=jnp.float32)
        * score_scale
    )
    visible = (key_pos[None, :] <= query_pos[:, None])[None, None]
    scores = jnp.where(visible, scores, big_negative)
    new_max = jnp.maximum(running_max, jnp.max(scores, axis=3))
    weights = jnp.where(visible, jnp.exp(scores - new_max[..., None]), 0.0)
    new_sum = jnp.sum(weights, axis=3)
    product = jnp.einsum(
        "gqtc,cgd->tgqd",
        weights.astype(jnp.bfloat16),
        value_heads,
        preferred_element_type=jnp.float32,
    )
    return (new_max, new_sum, product)


def run_expert(arrived, gate_up, down_weight):
    sources, slots, width = arrived.shape
    rows_in = arrived.reshape(sources * slots, width)
    projected = jnp.dot(rows_in, gate_up[0], preferred_element_type=jnp.float32)
    hidden_units = gate_up.shape[2] // 2
    hidden = (jax.nn.silu(projected[:, :hidden_units]) * projected[:, hidden_units:]).astype(
        jnp.bfloat16
    )
    result = jnp.dot(hidden, down_weight[0], preferred_element_type=jnp.float32).astype(
        jnp.bfloat16
    )
    return result.reshape(sources, slots, width)


def local(
    residual,
    queries,
    key_rows,
    value_rows,
    span_order,
    norm_gain,
    gate_logits,
    expert_ids,
    gate_up,
    down_weight,
):
    tokens_here = residual.shape[1]
    model_width = residual.shape[2]
    ctx_index = lax.axis_index("ctx")
    query_pos = span_positions(span_order, ctx_index * tokens_here, tokens_here)
    query_heads = queries[0].reshape(tokens_here, KVH, GROUP, HD)
    state_shape = (KVH, GROUP, tokens_here)
    initial = (
        jnp.full(state_shape, big_negative, jnp.float32),
        jnp.zeros(state_shape, jnp.float32),
        jnp.zeros((tokens_here, KVH, GROUP, HD), jnp.float32),
    )
    final_state = attend_update(
        initial,
        (
            lax.all_gather(key_rows, "ctx", axis=1, tiled=True),
            lax.all_gather(value_rows, "ctx", axis=1, tiled=True),
        ),
        jnp.int32(0),
        query_heads,
        query_pos,
        span_order,
    )
    running_sum = final_state[1]
    attention = (final_state[2] / jnp.transpose(running_sum, (2, 0, 1))[..., None]).reshape(
        tokens_here, -1
    )
    attention = lax.optimization_barrier(attention.astype(jnp.bfloat16)).astype(jnp.float32)
    mixed_rows = residual[0].astype(jnp.float32) + attention
    scale_rms = lax.rsqrt(jnp.mean(mixed_rows * mixed_rows, axis=1, keepdims=True) + norm_eps)
    normed = (mixed_rows * scale_rms * norm_gain).astype(jnp.bfloat16)
    raised = jnp.exp(gate_logits[0])
    routing_weight = raised / jnp.sum(raised, axis=1, keepdims=True)
    destinations = lax.axis_size("exp")
    top_count = expert_ids.shape[2]
    mean_load = tokens_here * top_count // destinations
    with_slack = mean_load + tokens_here * top_count // (4 * destinations)
    capacity = min(
        tokens_here, max(2, max(mean_load, min(with_slack, 524288 // (destinations * model_width))))
    )
    flat_experts = expert_ids[0].reshape(-1)
    owner_onehot = (
        flat_experts[:, None] == jnp.arange(destinations, dtype=jnp.int32)[None, :]
    ).astype(jnp.int32)
    earlier = jnp.cumsum(owner_onehot, axis=0) - owner_onehot
    slot_rank = jnp.sum(earlier * owner_onehot, axis=1)
    target_slot = flat_experts * capacity + slot_rank
    placement = (
        target_slot[:, None] == jnp.arange(destinations * capacity, dtype=jnp.int32)[None, :]
    ).astype(jnp.int32)
    token_map = placement.reshape(tokens_here, top_count, -1).sum(axis=1).astype(jnp.bfloat16)
    outgoing = jnp.einsum(
        "ts,td->sd", token_map, normed, preferred_element_type=jnp.float32
    ).astype(jnp.bfloat16)
    outgoing = outgoing.reshape(destinations, capacity, -1)
    arrived = lax.all_to_all(outgoing, "exp", split_axis=0, concat_axis=0, tiled=True)
    returned = lax.all_to_all(
        run_expert(arrived, gate_up, down_weight), "exp", split_axis=0, concat_axis=0, tiled=True
    )
    returned_rows = returned.reshape(destinations * capacity, -1)
    picked = (
        jnp.take(returned_rows, target_slot, axis=0)
        .astype(jnp.float32)
        .reshape(tokens_here, top_count, -1)
    )
    combined = jnp.sum(picked * routing_weight[:, :, None], axis=1)
    layer_out = (mixed_rows + combined).astype(jnp.bfloat16)
    return layer_out[None]


def solution(mesh):
    return jax.shard_map(
        local,
        mesh=mesh,
        in_specs=(
            P("exp", "ctx", None),
            P("exp", "ctx", None),
            P("exp", "ctx", None),
            P("exp", "ctx", None),
            P(),
            P(),
            P("exp", "ctx", None),
            P("exp", "ctx", None),
            P("exp", None, None),
            P("exp", None, None),
        ),
        out_specs=P("exp", "ctx", None),
        check_vma=False,
    )
```

profile of v0, /device:TPU:11, one launch (start us, length us, event | category | flops | bytes accessed | tf_op | source)
XLA Modules:
  0.0 144.3 jit_solution(2318185665745731534)
XLA Ops:
  0.0 0.0 copy-start
  0.0 0.9 copy.54
  0.9 0.1 eq.76
  1.0 0.1 reshape_squeeze.15
  1.1 0.7 select_reduce_fusion
  1.9 0.7 select_reduce_fusion.1
  2.6 1.0 copy.69
  3.6 3.6 %all_gather.6 = bf16[1,128,256]{2,1,0:T(8,128)(2,1)S(1)} all-gather(bf16[1,64,256]{2,1,0:T(8,128)(2,1)} %param.12), channel_id=1, replica_groups=mesh['ctx'=2,'exp'=16] {'ctx'}, dimensions={1}, use_global_device_ids=true | all-gather | bytes 98304 | tf_op jit(solution)/shard_map/all_gather | solution.py:90
  7.3 0.1 copy.48
  7.4 0.1 broadcast_compare_fusion
  7.5 1.0 fusion.30
  8.5 3.6 %all_gather.7 = bf16[1,128,256]{2,1,0:T(8,128)(2,1)S(1)} all-gather(bf16[1,64,256]{2,1,0:T(8,128)(2,1)} %param.13), channel_id=1, replica_groups=mesh['ctx'=2,'exp'=16] {'ctx'}, dimensions={1}, use_global_device_ids=true | all-gather | bytes 98304 | tf_op jit(solution)/shard_map/all_gather | solution.py:91
  12.1 0.1 copy.51
  12.2 0.0 copy-start.1
  12.2 1.5 %fusion.8 = f32[2,8,64]{2,1,0:T(8,128)S(1)} fusion(f32[2,8,64,128]{3,2,1,0:T(8,128)} %get-tuple-element.8, f32[2,8,64]{2,1,0:T(8,128)S(1)} %broadcast_maximum_fusion, pred[64,128]{1,0:T(8,128)(4,1)S(1)} %broadcast_compare_fusion), kind=kLoop, calls=%fused_computation.23 | loop fusion | flops 392192 | bytes 540672 | tf_op jit(solution)/shard_map/reduce_sum | solution.py:40
  13.7 0.0 copy-start.3
  13.8 0.0 copy-start.5
  13.8 1.4 fusion.6
  15.2 0.2 copy.53
  15.4 0.1 copy.77
  15.4 0.0 copy-done.1
  15.4 0.2 multiply_reduce_fusion.1
  15.7 1.2 reduce-window.6
  16.8 0.2 slice_reduce_fusion
  17.1 0.1 fusion.24
  17.2 0.1 reduce_sum.80
  17.3 0.1 copy.57
  17.3 0.0 copy-done.3
  17.3 0.1 copy.59
  17.4 0.4 convert_reduce_fusion
  17.8 0.0 copy-done.5
  17.8 1.7 %convolution_convert_fusion.1 = bf16[512,2048]{1,0:T(8,128)(2,1)S(1)} fusion(bf16[64,2048]{1,0:T(8,128)(2,1)S(1)} %bitcast.85, bf16[1,64,2048]{2,1,0:T(8,128)(2,1)} %param.10, f32[2048]{0:T(1024)S(1)} %copy-done.5, f32[64]{0:T(128)S(1)} %add_rsqrt_fusion, s32[64,512]{1,0:T(8,128)S(1)} %convert_reduce_fusion), kind=kOutput, calls=%fused_computation.5 | convolution fusion | flops 136085504 | bytes 2760960 | tf_op jit(solution)/shard_map/ts,td->sd/dot_general | solution.py:126
  19.5 55.9 %all_to_all.10 = bf16[16,32,2048]{2,1,0:T(8,128)(2,1)S(1)} all-to-all(bf16[16,32,2048]{2,1,0:T(8,128)(2,1)S(1)} %bitcast.83), channel_id=1, replica_groups=mesh['ctx'=2,'exp'=16] {'exp'}, dimensions={0} | all-to-all | bytes 4194304 | tf_op jit(solution)/shard_map/all_to_all | solution.py:130
  75.4 0.0 copy-done
  75.4 0.0 copy-start.6
  75.4 1.8 %fusion = f32[512,768]{1,0:T(8,128)S(1)} fusion(bf16[512,2048]{1,0:T(8,128)(2,1)S(1)} %bitcast.88, bf16[1,2048,768]{2,1,0:T(8,128)(2,1)S(1)} %copy-done), kind=kOutput, calls=%fused_computation.2 | convolution fusion | flops 1610612736 | bytes 6815744 | tf_op jit(solution)/shard_map/dot_general | solution.py:53
  77.2 0.0 copy-done.6
  77.2 2.6 %convolution_convert_fusion = bf16[512,2048]{1,0:T(8,128)(2,1)} fusion(bf16[1,384,2048]{2,1,0:T(8,128)(2,1)S(1)} %copy-done.6, f32[512,768]{1,0:T(8,128)S(1)} %fusion), kind=kOutput, calls=%fused_computation.4 | convolution fusion | flops 807534592 | bytes 5242880 | tf_op jit(solution)/shard_map/dot_general | solution.py:58
  79.8 0.0 copy-start.4
  79.8 5.2 %all-to-all-start.1 = ((bf16[16,32,2048]{2,1,0:T(8,128)(2,1)}), bf16[16,32,2048]{2,1,0:T(8,128)(2,1)}, u32[]{:S(2)}, u32[]{:S(2)}) async-start(bf16[16,32,2048]{2,1,0:T(8,128)(2,1)} %bitcast.87), calls=%async_computation.1 | async-start | bytes 4194304 | tf_op jit(solution)/shard_map/all_to_all | solution.py:131
  85.0 0.1 copy.60
  85.1 0.1 mul.107
  85.2 0.1 copy.58
  85.3 0.0 copy-done.4
  85.3 0.1 copy.61
  85.4 47.1 %all-to-all-done.1 = bf16[16,32,2048]{2,1,0:T(8,128)(2,1)} async-done(((bf16[16,32,2048]{2,1,0:T(8,128)(2,1)}), bf16[16,32,2048]{2,1,0:T(8,128)(2,1)}, u32[]{:S(2)}, u32[]{:S(2)}) %all-to-all-start.1) | async-done | bytes 2097184 | tf_op jit(solution)/shard_map/all_to_all | solution.py:131
  132.5 7.1 %gather_fusion = bf16[512,2048]{1,0:T(8,128)(2,1)} fusion(bf16[512,2048]{1,0:T(8,128)(2,1)} %bitcast.15, s32[1024]{0:T(1024)S(1)} %pad_clamp_fusion), kind=kCustom, calls=%fused_computation | custom fusion | bytes 4196352 | tf_op jit(solution)/shard_map/jit(_take)/gather | solution.py:136
  139.6 0.0 copy-start.2
  139.6 3.9 %multiply_reduce_fusion = f32[64,2048]{1,0:T(8,128)S(1)} fusion(bf16[512,2048]{1,0:T(8,128)(2,1)} %gather_fusion, f32[64,8]{1,0:T(8,128)S(1)} %copy.61, pred[64,8]{1,0:T(8,128)(4,1)S(1)} %copy.58), kind=kLoop, calls=%fused_computation.1 | loop fusion | flops 4063232 | bytes 2624000 | tf_op jit(solution)/shard_map/reduce_sum | solution.py:140
  143.5 0.0 copy-done.2
  143.5 0.8 fusion.13
  (15 shorter events, 0.2 us)
Async XLA Ops:
  0.0 75.4 %copy-start = (bf16[1,2048,768]{2,1,0:T(8,128)(2,1)S(1)}, bf16[1,2048,768]{2,1,0:T(8,128)(2,1)}, u32[]{:S(2)}) copy-start(bf16[1,2048,768]{2,1,0:T(8,128)(2,1)} %param.18) | copy-start | bytes 9437188
  12.2 3.2 %copy-start.1 = (bf16[1,64,2048]{2,1,0:T(8,128)(2,1)S(1)}, bf16[1,64,2048]{2,1,0:T(8,128)(2,1)}, u32[]{:S(2)}) copy-start(bf16[1,64,2048]{2,1,0:T(8,128)(2,1)} %param.10) | copy-start | bytes 786436
  13.7 3.6 %copy-start.3 = (s32[1,64,8]{1,2,0:T(8,128)S(1)}, s32[1,64,8]{1,2,0:T(8,128)}, u32[]{:S(2)}) copy-start(s32[1,64,8]{1,2,0:T(8,128)} %param.17) | copy-start | bytes 6148
  13.8 4.1 %copy-start.5 = (f32[2048]{0:T(1024)S(1)}, f32[2048]{0:T(1024)}, u32[]{:S(2)}) copy-start(f32[2048]{0:T(1024)} %param.15) | copy-start | bytes 24580
  75.4 1.8 %copy-start.6 = (bf16[1,384,2048]{2,1,0:T(8,128)(2,1)S(1)}, bf16[1,384,2048]{2,1,0:T(8,128)(2,1)}, u32[]{:S(2)}) copy-start(bf16[1,384,2048]{2,1,0:T(8,128)(2,1)} %param.19) | copy-start | bytes 4718596
  79.8 5.5 %copy-start.4 = (f32[1,64,8]{1,2,0:T(8,128)S(1)}, f32[1,64,8]{1,2,0:T(8,128)}, u32[]{:S(2)}) copy-start(f32[1,64,8]{1,2,0:T(8,128)} %param.16) | copy-start | bytes 6148
  79.8 52.7 %all-to-all-start.1 = ((bf16[16,32,2048]{2,1,0:T(8,128)(2,1)}), bf16[16,32,2048]{2,1,0:T(8,128)(2,1)}, u32[]{:S(2)}, u32[]{:S(2)}) async-start(bf16[16,32,2048]{2,1,0:T(8,128)(2,1)} %bitcast.87), calls=%async_computation.1 | async-start | bytes 4194304 | tf_op jit(solution)/shard_map/all_to_all | solution.py:131
  139.6 3.9 %copy-start.2 = (bf16[1,64,2048]{2,1,0:T(8,128)(2,1)S(1)}, bf16[1,64,2048]{2,1,0:T(8,128)(2,1)}, u32[]{:S(2)}) copy-start(bf16[1,64,2048]{2,1,0:T(8,128)(2,1)} %param.10) | copy-start | bytes 786436
where the time goes:
time: 145 us; the launch traced here: 144 us
  blocking collectives  63.2 us (44%)
  waiting for transfers between devices  47.1 us (32%)
  local copies, waits for them, and re-layouts  10.5 us (7%)
  other arithmetic  9.65 us (7%)
  matrix products  8.49 us (6%)
  starting transfers between devices  5.17 us (4%)
    all_to_all x1, blocking collectives, local(): lax.all_to_all(outgoing, 'exp', split_axis=0, concat_axis=0, tiled=True)  55.9 us
    all_to_all x1, waiting for transfers between devices, local(): lax.all_to_all(run_expert(arrived, gate_up, down_weight), 'exp', split_ax...  47.1 us
    gather x1, local copies, waits for them, and re-layouts, local(): jnp.take(returned_rows, target_slot, axis=0).astype(jnp.float32)  7.1 us
    all_to_all x1, starting transfers between devices, local(): lax.all_to_all(run_expert(arrived, gate_up, down_weight), 'exp', split_ax...  5.17 us
    reduce_sum x1, other arithmetic, local(): combined = jnp.sum(picked * routing_weight[:, :, None], axis=1)  3.86 us
    all_gather x1, blocking collectives, local(): lax.all_gather(key_rows, 'ctx', axis=1, tiled=True)  3.64 us
    all_gather x1, blocking collectives, local(): lax.all_gather(value_rows, 'ctx', axis=1, tiled=True)  3.63 us
  transfers between devices with their start and end apart: 1, of which 1 were waited for; matrix products, arithmetic and copies ran while one was open for 0% of the time, Pallas kernels for 0%

commit v1 on v0

--- a/solution.py
+++ b/solution.py
@@ -1,3 +1,4 @@
+import functools
 import math
 import jax
 import jax.numpy as jnp
@@ -10,6 +11,29 @@
 HALF = 32
 big_negative = -1e30
 norm_eps = 1e-06
+
+
+def _direct_weights(unit, axis_k, d_out):
+    w2, m_next = (lax.axis_size("exp"), lax.axis_index("exp"))
+    state_now = unit.shape[axis_k] // w2
+    arr_next = list(unit.shape)
+    arr_next[axis_k] = state_now
+    finding = arr_next[d_out]
+    arr_next[d_out] = finding * w2
+    later = jnp.zeros(arr_next, unit.dtype)
+    q = 0
+    while q < w2:
+        carry_out = lax.dynamic_slice_in_dim(unit, (m_next ^ q) * state_now, state_now, axis=axis_k)
+        if q:
+            carry_out = lax.ppermute(carry_out, "exp", tuple(((i, i ^ q) for i in range(w2))))
+        later = lax.dynamic_update_slice_in_dim(
+            later, carry_out, (m_next ^ q) * finding, axis=d_out
+        )
+        q = q + 1
+    return later
+
+
+run_numbers = functools.partial(_direct_weights, axis_k=0, d_out=0)
 
 
 def span_positions(span_order, first_row, row_total):
@@ -127,7 +151,7 @@
         "ts,td->sd", token_map, normed, preferred_element_type=jnp.float32
     ).astype(jnp.bfloat16)
     outgoing = outgoing.reshape(destinations, capacity, -1)
-    arrived = lax.all_to_all(outgoing, "exp", split_axis=0, concat_axis=0, tiled=True)
+    arrived = run_numbers(outgoing)
     returned = lax.all_to_all(
         run_expert(arrived, gate_up, down_weight), "exp", split_axis=0, concat_axis=0, tiled=True
     )

time: 145 us -> 153 us (1.055)
  blocking collectives: 63.2 us -> 7.27 us
  waiting for transfers between devices: 47.1 us -> 83.8 us
  starting transfers between devices: 5.17 us -> 28.3 us
  local copies, waits for them, and re-layouts: 10.5 us -> 12.5 us
  other arithmetic: 9.65 us -> 11.6 us
    all_to_all x1 -> x0, blocking collectives: 55.9 us -> none  [local(): lax.all_to_all(outgoing, 'exp', split_axis=0, concat_axis=0, tiled=True)]
    ppermute x0 -> x15, waiting for transfers between devices: none -> 36.6 us  [_direct_weights(): lax.ppermute(carry_out, 'exp', tuple(((i, i ^ q) for i in range(w2))))]
    ppermute x0 -> x15, starting transfers between devices: none -> 22.1 us  [_direct_weights(): lax.ppermute(carry_out, 'exp', tuple(((i, i ^ q) for i in range(w2))))]
  transfers between devices with their start and end apart: 1 -> 16, of which waited for: 1 -> 10; matrix products, arithmetic and copies ran while one was open for 0% -> 0% of each run, Pallas kernels for 0% -> 0%
where the time goes in v1:
time: 153 us; the launch traced here: 152 us
  waiting for transfers between devices  83.8 us (55%)
  starting transfers between devices  28.3 us (18%)
  local copies, waits for them, and re-layouts  12.5 us (8%)
  other arithmetic  11.6 us (8%)
  matrix products  8.5 us (6%)
  blocking collectives  7.27 us (5%)
    all_to_all x1, waiting for transfers between devices, local(): lax.all_to_all(run_expert(arrived, gate_up, down_weight), 'exp', split_ax...  47.2 us
    ppermute x15, waiting for transfers between devices, _direct_weights(): lax.ppermute(carry_out, 'exp', tuple(((i, i ^ q) for i in range(w2))))  36.6 us
    ppermute x15, starting transfers between devices, _direct_weights(): lax.ppermute(carry_out, 'exp', tuple(((i, i ^ q) for i in range(w2))))  22.1 us
    gather x1, local copies, waits for them, and re-layouts, local(): jnp.take(returned_rows, target_slot, axis=0).astype(jnp.float32)  7.1 us
    all_to_all x1, starting transfers between devices, local(): lax.all_to_all(run_expert(arrived, gate_up, down_weight), 'exp', split_ax...  6.18 us
    reduce_sum x1, other arithmetic, local(): combined = jnp.sum(picked * routing_weight[:, :, None], axis=1)  3.86 us
    all_gather x1, blocking collectives, local(): lax.all_gather(key_rows, 'ctx', axis=1, tiled=True)  3.64 us
    all_gather x1, blocking collectives, local(): lax.all_gather(value_rows, 'ctx', axis=1, tiled=True)  3.63 us
  transfers between devices with their start and end apart: 16, of which 10 were waited for; matrix products, arithmetic and copies ran while one was open for 0% of the time, Pallas kernels for 0%

profile of v1, /device:TPU:11, one launch (start us, length us, event | category | flops | bytes accessed | tf_op | source)
XLA Modules:
  0.0 152.3 jit_solution(14142427187691413353)
XLA Ops:
  0.0 0.9 copy.54
  0.9 0.1 eq.76
  1.0 0.7 reshape_squeeze.15
  1.7 0.7 select_reduce_fusion
  2.5 0.7 select_reduce_fusion.1
  3.2 1.0 copy.69
  4.2 3.6 %all_gather.6 = bf16[1,128,256]{2,1,0:T(8,128)(2,1)S(1)} all-gather(bf16[1,64,256]{2,1,0:T(8,128)(2,1)} %param.12), channel_id=1, replica_groups=mesh['ctx'=2,'exp'=16] {'ctx'}, dimensions={1}, use_global_device_ids=true | all-gather | bytes 98304 | tf_op jit(solution)/shard_map/all_gather | solution.py:114
  7.8 0.1 copy.48
  8.0 0.1 broadcast_compare_fusion
  8.0 1.0 fusion.30
  9.1 3.6 %all_gather.7 = bf16[1,128,256]{2,1,0:T(8,128)(2,1)S(1)} all-gather(bf16[1,64,256]{2,1,0:T(8,128)(2,1)} %param.13), channel_id=1, replica_groups=mesh['ctx'=2,'exp'=16] {'ctx'}, dimensions={1}, use_global_device_ids=true | all-gather | bytes 98304 | tf_op jit(solution)/shard_map/all_gather | solution.py:115
  12.7 0.1 copy.51
  12.8 0.0 copy-start.1
  12.8 1.5 fusion.8
  14.3 0.0 copy-start.3
  14.3 1.4 fusion.6
  15.8 0.2 copy.53
  15.9 0.1 copy.77
  16.0 0.2 multiply_reduce_fusion.1
  16.2 0.6 add_rsqrt_fusion
  16.8 1.1 reduce-window.6
  18.0 0.2 slice_reduce_fusion
  18.2 0.1 fusion.24
  18.3 0.1 reduce_sum.80
  18.4 0.1 copy.57
  18.5 0.6 compare_and_fusion
  19.1 0.7 copy.59
  19.8 1.1 convert_reduce_fusion
  21.0 1.7 %convolution_convert_fusion.1 = bf16[512,2048]{1,0:T(8,128)(2,1)S(1)} fusion(bf16[64,2048]{1,0:T(8,128)(2,1)S(1)} %bitcast.85, bf16[1,64,2048]{2,1,0:T(8,128)(2,1)} %param.10, f32[2048]{0:T(1024)S(1)} %copy-done.5, f32[64]{0:T(128)} %add_rsqrt_fusion, s32[64,512]{1,0:T(8,128)S(1)} %convert_reduce_fusion), kind=kOutput, calls=%fused_computation.5 | convolution fusion | flops 136085504 | bytes 2760960 | tf_op jit(solution)/shard_map/ts,td->sd/dot_general | solution.py:150
  22.7 0.2 broadcast_in_dim.88
  23.0 0.3 constant_dynamic-slice_fusion
  23.3 3.0 %collective-permute-start = (bf16[1,32,2048]{2,1,0:T(8,128)(2,1)S(1)}, bf16[1,32,2048]{2,1,0:T(8,128)(2,1)S(1)}, u32[]{:S(2)}, u32[]{:S(2)}) collective-permute-start(bf16[1,32,2048]{2,1,0:T(8,128)(2,1)S(1)} %get-tuple-element.21), channel_id=1, source_target_pairs={{0,1},{1,0},{2,3},{3,2},{4,5},{5,4},{6,7},{7,6},{8,9},{9,8},{10,11... | collective-permute-start | bytes 393224 | tf_op jit(solution)/shard_map/ppermute | solution.py:28
  26.4 0.3 collective-permute-start.1
  26.6 1.5 collective-permute-start.2
  28.1 0.2 collective-permute-start.3
  28.2 1.6 %collective-permute-start.4 = (bf16[1,32,2048]{2,1,0:T(8,128)(2,1)S(1)}, bf16[1,32,2048]{2,1,0:T(8,128)(2,1)S(1)}, u32[]{:S(2)}, u32[]{:S(2)}) collective-permute-start(bf16[1,32,2048]{2,1,0:T(8,128)(2,1)S(1)} %get-tuple-element.17), channel_id=1, source_target_pairs={{0,5},{1,4},{2,7},{3,6},{4,1},{5,0},{6,3},{7,2},{8,13},{9,12},{10,... | collective-permute-start | bytes 393224 | tf_op jit(solution)/shard_map/ppermute | solution.py:28
  29.9 1.5 collective-permute-done.1
  31.3 1.2 collective-permute-start.6
  32.6 2.1 %collective-permute-done.2 = bf16[1,32,2048]{2,1,0:T(8,128)(2,1)S(1)} collective-permute-done((bf16[1,32,2048]{2,1,0:T(8,128)(2,1)S(1)}, bf16[1,32,2048]{2,1,0:T(8,128)(2,1)S(1)}, u32[]{:S(2)}, u32[]{:S(2)}) %collective-permute-start.2) | collective-permute-done | bytes 131104 | tf_op jit(solution)/shard_map/ppermute | solution.py:28
  34.7 2.3 %collective-permute-start.7 = (bf16[1,32,2048]{2,1,0:T(8,128)(2,1)S(1)}, bf16[1,32,2048]{2,1,0:T(8,128)(2,1)S(1)}, u32[]{:S(2)}, u32[]{:S(2)}) collective-permute-start(bf16[1,32,2048]{2,1,0:T(8,128)(2,1)S(1)} %get-tuple-element.14), channel_id=1, source_target_pairs={{0,8},{1,9},{2,10},{3,11},{4,12},{5,13},{6,14},{7,15},{8,0},{9,1},... | collective-permute-start | bytes 393224 | tf_op jit(solution)/shard_map/ppermute | solution.py:28
  37.0 0.1 collective-permute-start.8
  37.2 2.3 %collective-permute-start.9 = (bf16[1,32,2048]{2,1,0:T(8,128)(2,1)S(1)}, bf16[1,32,2048]{2,1,0:T(8,128)(2,1)S(1)}, u32[]{:S(2)}, u32[]{:S(2)}) collective-permute-start(bf16[1,32,2048]{2,1,0:T(8,128)(2,1)S(1)} %get-tuple-element.12), channel_id=1, source_target_pairs={{0,10},{1,11},{2,8},{3,9},{4,14},{5,15},{6,12},{7,13},{8,2},{9,3},... | collective-permute-start | bytes 393224 | tf_op jit(solution)/shard_map/ppermute | solution.py:28
  39.6 7.3 %collective-permute-start.10 = (bf16[1,32,2048]{2,1,0:T(8,128)(2,1)S(1)}, bf16[1,32,2048]{2,1,0:T(8,128)(2,1)S(1)}, u32[]{:S(2)}, u32[]{:S(2)}) collective-permute-start(bf16[1,32,2048]{2,1,0:T(8,128)(2,1)S(1)} %get-tuple-element.11), channel_id=1, source_target_pairs={{0,11},{1,10},{2,9},{3,8},{4,15},{5,14},{6,13},{7,12},{8,3},{9,2},... | collective-permute-start | bytes 393224 | tf_op jit(solution)/shard_map/ppermute | solution.py:28
  46.9 1.4 collective-permute-start.11
  48.3 0.1 collective-permute-start.12
  48.4 11.3 %collective-permute-done.8 = bf16[1,32,2048]{2,1,0:T(8,128)(2,1)S(1)} collective-permute-done((bf16[1,32,2048]{2,1,0:T(8,128)(2,1)S(1)}, bf16[1,32,2048]{2,1,0:T(8,128)(2,1)S(1)}, u32[]{:S(2)}, u32[]{:S(2)}) %collective-permute-start.8) | collective-permute-done | bytes 131104 | tf_op jit(solution)/shard_map/ppermute | solution.py:28
  59.7 2.8 %collective-permute-done.9 = bf16[1,32,2048]{2,1,0:T(8,128)(2,1)S(1)} collective-permute-done((bf16[1,32,2048]{2,1,0:T(8,128)(2,1)S(1)}, bf16[1,32,2048]{2,1,0:T(8,128)(2,1)S(1)}, u32[]{:S(2)}, u32[]{:S(2)}) %collective-permute-start.9) | collective-permute-done | bytes 131104 | tf_op jit(solution)/shard_map/ppermute | solution.py:28
  62.5 0.8 collective-permute-start.14
  63.4 4.6 %collective-permute-done.10 = bf16[1,32,2048]{2,1,0:T(8,128)(2,1)S(1)} collective-permute-done((bf16[1,32,2048]{2,1,0:T(8,128)(2,1)S(1)}, bf16[1,32,2048]{2,1,0:T(8,128)(2,1)S(1)}, u32[]{:S(2)}, u32[]{:S(2)}) %collective-permute-start.10) | collective-permute-done | bytes 131104 | tf_op jit(solution)/shard_map/ppermute | solution.py:28
  68.0 5.7 %collective-permute-done.11 = bf16[1,32,2048]{2,1,0:T(8,128)(2,1)S(1)} collective-permute-done((bf16[1,32,2048]{2,1,0:T(8,128)(2,1)S(1)}, bf16[1,32,2048]{2,1,0:T(8,128)(2,1)S(1)}, u32[]{:S(2)}, u32[]{:S(2)}) %collective-permute-start.11) | collective-permute-done | bytes 131104 | tf_op jit(solution)/shard_map/ppermute | solution.py:28
  73.8 2.9 %collective-permute-done.12 = bf16[1,32,2048]{2,1,0:T(8,128)(2,1)S(1)} collective-permute-done((bf16[1,32,2048]{2,1,0:T(8,128)(2,1)S(1)}, bf16[1,32,2048]{2,1,0:T(8,128)(2,1)S(1)}, u32[]{:S(2)}, u32[]{:S(2)}) %collective-permute-start.12) | collective-permute-done | bytes 131104 | tf_op jit(solution)/shard_map/ppermute | solution.py:28
  76.7 2.8 %collective-permute-done.13 = bf16[1,32,2048]{2,1,0:T(8,128)(2,1)S(1)} collective-permute-done((bf16[1,32,2048]{2,1,0:T(8,128)(2,1)S(1)}, bf16[1,32,2048]{2,1,0:T(8,128)(2,1)S(1)}, u32[]{:S(2)}, u32[]{:S(2)}) %collective-permute-start.13) | collective-permute-done | bytes 131104 | tf_op jit(solution)/shard_map/ppermute | solution.py:28
  79.5 2.8 %collective-permute-done.14 = bf16[1,32,2048]{2,1,0:T(8,128)(2,1)S(1)} collective-permute-done((bf16[1,32,2048]{2,1,0:T(8,128)(2,1)S(1)}, bf16[1,32,2048]{2,1,0:T(8,128)(2,1)S(1)}, u32[]{:S(2)}, u32[]{:S(2)}) %collective-permute-start.14) | collective-permute-done | bytes 131104 | tf_op jit(solution)/shard_map/ppermute | solution.py:28
  82.3 1.8 %fusion = f32[512,768]{1,0:T(8,128)S(1)} fusion(bf16[512,2048]{1,0:T(8,128)(2,1)S(1)} %bitcast.87, bf16[1,2048,768]{2,1,0:T(8,128)(2,1)S(1)} %copy-done), kind=kOutput, calls=%fused_computation.2 | convolution fusion | flops 1610612736 | bytes 6815744 | tf_op jit(solution)/shard_map/dot_general | solution.py:77
  84.1 2.6 %convolution_convert_fusion = bf16[512,2048]{1,0:T(8,128)(2,1)} fusion(bf16[1,384,2048]{2,1,0:T(8,128)(2,1)S(1)} %copy-done.8, f32[512,768]{1,0:T(8,128)S(1)} %fusion), kind=kOutput, calls=%fused_computation.4 | convolution fusion | flops 807534592 | bytes 5242880 | tf_op jit(solution)/shard_map/dot_general | solution.py:82
  86.7 6.2 %all-to-all-start = ((bf16[16,32,2048]{2,1,0:T(8,128)(2,1)}), bf16[16,32,2048]{2,1,0:T(8,128)(2,1)}, u32[]{:S(2)}, u32[]{:S(2)}) async-start(bf16[16,32,2048]{2,1,0:T(8,128)(2,1)} %bitcast.88), calls=%async_computation | async-start | bytes 4194304 | tf_op jit(solution)/shard_map/all_to_all | solution.py:155
  92.9 0.1 copy.60
  93.0 0.1 mul.107
  93.1 0.1 copy.58
  93.2 0.1 copy.61
  93.3 47.2 %all-to-all-done = bf16[16,32,2048]{2,1,0:T(8,128)(2,1)} async-done(((bf16[16,32,2048]{2,1,0:T(8,128)(2,1)}), bf16[16,32,2048]{2,1,0:T(8,128)(2,1)}, u32[]{:S(2)}, u32[]{:S(2)}) %all-to-all-start) | async-done | bytes 2097184 | tf_op jit(solution)/shard_map/all_to_all | solution.py:155
  140.5 7.1 %gather_fusion = bf16[512,2048]{1,0:T(8,128)(2,1)} fusion(bf16[512,2048]{1,0:T(8,128)(2,1)} %bitcast.15, s32[1024]{0:T(1024)S(1)} %pad_clamp_fusion), kind=kCustom, calls=%fused_computation | custom fusion | bytes 4196352 | tf_op jit(solution)/shard_map/jit(_take)/gather | solution.py:160
  147.6 3.9 %multiply_reduce_fusion = f32[64,2048]{1,0:T(8,128)S(1)} fusion(bf16[512,2048]{1,0:T(8,128)(2,1)} %gather_fusion, f32[64,8]{1,0:T(8,128)S(1)} %copy.61, pred[64,8]{1,0:T(8,128)(4,1)S(1)} %copy.58), kind=kLoop, calls=%fused_computation.1 | loop fusion | flops 4063232 | bytes 2624000 | tf_op jit(solution)/shard_map/reduce_sum | solution.py:164
  151.5 0.8 fusion.13
  (52 shorter events, 0.4 us)
Async XLA Ops:
  0.0 82.3 %copy-start = (bf16[1,2048,768]{2,1,0:T(8,128)(2,1)S(1)}, bf16[1,2048,768]{2,1,0:T(8,128)(2,1)}, u32[]{:S(2)}) copy-start(bf16[1,2048,768]{2,1,0:T(8,128)(2,1)} %param.18) | copy-start | bytes 9437188
  12.8 3.2 %copy-start.1 = (bf16[1,64,2048]{2,1,0:T(8,128)(2,1)S(1)}, bf16[1,64,2048]{2,1,0:T(8,128)(2,1)}, u32[]{:S(2)}) copy-start(bf16[1,64,2048]{2,1,0:T(8,128)(2,1)} %param.10) | copy-start | bytes 786436
  14.3 3.9 %copy-start.6 = (s32[512]{0:T(512)S(1)}, s32[512]{0:T(512)}, u32[]{:S(2)}) copy-start(s32[512]{0:T(512)} %reshape_squeeze.15) | copy-start | bytes 6148
  14.3 4.2 %copy-start.3 = (s32[1,64,8]{1,2,0:T(8,128)S(1)}, s32[1,64,8]{1,2,0:T(8,128)}, u32[]{:S(2)}) copy-start(s32[1,64,8]{1,2,0:T(8,128)} %param.17) | copy-start | bytes 6148
  14.3 6.7 %copy-start.5 = (f32[2048]{0:T(1024)S(1)}, f32[2048]{0:T(1024)}, u32[]{:S(2)}) copy-start(f32[2048]{0:T(1024)} %param.15) | copy-start | bytes 24580
  23.3 6.5 %collective-permute-start = (bf16[1,32,2048]{2,1,0:T(8,128)(2,1)S(1)}, bf16[1,32,2048]{2,1,0:T(8,128)(2,1)S(1)}, u32[]{:S(2)}, u32[]{:S(2)}) collective-permute-start(bf16[1,32,2048]{2,1,0:T(8,128)(2,1)S(1)} %get-tuple-element.21), channel_id=1, source_target_pairs={{0,1},{1,0},{2,3},{3,2},{4,5},{5,4},{6,7},{7,6},{8,9},{9,8},{10,11... | collective-permute-start | bytes 393224 | tf_op jit(solution)/shard_map/ppermute | solution.py:28
  26.4 5.0 %collective-permute-start.1 = (bf16[1,32,2048]{2,1,0:T(8,128)(2,1)S(1)}, bf16[1,32,2048]{2,1,0:T(8,128)(2,1)S(1)}, u32[]{:S(2)}, u32[]{:S(2)}) collective-permute-start(bf16[1,32,2048]{2,1,0:T(8,128)(2,1)S(1)} %get-tuple-element.20), channel_id=1, source_target_pairs={{0,2},{1,3},{2,0},{3,1},{4,6},{5,7},{6,4},{7,5},{8,10},{9,11},{10,... | collective-permute-start | bytes 393224 | tf_op jit(solution)/shard_map/ppermute | solution.py:28
  26.6 8.1 %collective-permute-start.2 = (bf16[1,32,2048]{2,1,0:T(8,128)(2,1)S(1)}, bf16[1,32,2048]{2,1,0:T(8,128)(2,1)S(1)}, u32[]{:S(2)}, u32[]{:S(2)}) collective-permute-start(bf16[1,32,2048]{2,1,0:T(8,128)(2,1)S(1)} %get-tuple-element.19), channel_id=1, source_target_pairs={{0,3},{1,2},{2,1},{3,0},{4,7},{5,6},{6,5},{7,4},{8,11},{9,10},{10,... | collective-permute-start | bytes 393224 | tf_op jit(solution)/shard_map/ppermute | solution.py:28
  28.1 8.9 %collective-permute-start.3 = (bf16[1,32,2048]{2,1,0:T(8,128)(2,1)S(1)}, bf16[1,32,2048]{2,1,0:T(8,128)(2,1)S(1)}, u32[]{:S(2)}, u32[]{:S(2)}) collective-permute-start(bf16[1,32,2048]{2,1,0:T(8,128)(2,1)S(1)} %get-tuple-element.18), channel_id=1, source_target_pairs={{0,4},{1,5},{2,6},{3,7},{4,0},{5,1},{6,2},{7,3},{8,12},{9,13},{10,... | collective-permute-start | bytes 393224 | tf_op jit(solution)/shard_map/ppermute | solution.py:28
  28.2 8.9 %collective-permute-start.4 = (bf16[1,32,2048]{2,1,0:T(8,128)(2,1)S(1)}, bf16[1,32,2048]{2,1,0:T(8,128)(2,1)S(1)}, u32[]{:S(2)}, u32[]{:S(2)}) collective-permute-start(bf16[1,32,2048]{2,1,0:T(8,128)(2,1)S(1)} %get-tuple-element.17), channel_id=1, source_target_pairs={{0,5},{1,4},{2,7},{3,6},{4,1},{5,0},{6,3},{7,2},{8,13},{9,12},{10,... | collective-permute-start | bytes 393224 | tf_op jit(solution)/shard_map/ppermute | solution.py:28
  29.9 9.7 %collective-permute-start.5 = (bf16[1,32,2048]{2,1,0:T(8,128)(2,1)S(1)}, bf16[1,32,2048]{2,1,0:T(8,128)(2,1)S(1)}, u32[]{:S(2)}, u32[]{:S(2)}) collective-permute-start(bf16[1,32,2048]{2,1,0:T(8,128)(2,1)S(1)} %get-tuple-element.16), channel_id=1, source_target_pairs={{0,6},{1,7},{2,4},{3,5},{4,2},{5,3},{6,0},{7,1},{8,14},{9,15},{10,... | collective-permute-start | bytes 393224 | tf_op jit(solution)/shard_map/ppermute | solution.py:28
  31.3 15.5 %collective-permute-start.6 = (bf16[1,32,2048]{2,1,0:T(8,128)(2,1)S(1)}, bf16[1,32,2048]{2,1,0:T(8,128)(2,1)S(1)}, u32[]{:S(2)}, u32[]{:S(2)}) collective-permute-start(bf16[1,32,2048]{2,1,0:T(8,128)(2,1)S(1)} %get-tuple-element.15), channel_id=1, source_target_pairs={{0,7},{1,6},{2,5},{3,4},{4,3},{5,2},{6,1},{7,0},{8,15},{9,14},{10,... | collective-permute-start | bytes 393224 | tf_op jit(solution)/shard_map/ppermute | solution.py:28
  34.7 13.6 %collective-permute-start.7 = (bf16[1,32,2048]{2,1,0:T(8,128)(2,1)S(1)}, bf16[1,32,2048]{2,1,0:T(8,128)(2,1)S(1)}, u32[]{:S(2)}, u32[]{:S(2)}) collective-permute-start(bf16[1,32,2048]{2,1,0:T(8,128)(2,1)S(1)} %get-tuple-element.14), channel_id=1, source_target_pairs={{0,8},{1,9},{2,10},{3,11},{4,12},{5,13},{6,14},{7,15},{8,0},{9,1},... | collective-permute-start | bytes 393224 | tf_op jit(solution)/shard_map/ppermute | solution.py:28
  37.0 22.7 %collective-permute-start.8 = (bf16[1,32,2048]{2,1,0:T(8,128)(2,1)S(1)}, bf16[1,32,2048]{2,1,0:T(8,128)(2,1)S(1)}, u32[]{:S(2)}, u32[]{:S(2)}) collective-permute-start(bf16[1,32,2048]{2,1,0:T(8,128)(2,1)S(1)} %get-tuple-element.13), channel_id=1, source_target_pairs={{0,9},{1,8},{2,11},{3,10},{4,13},{5,12},{6,15},{7,14},{8,1},{9,0},... | collective-permute-start | bytes 393224 | tf_op jit(solution)/shard_map/ppermute | solution.py:28
  37.2 25.3 %collective-permute-start.9 = (bf16[1,32,2048]{2,1,0:T(8,128)(2,1)S(1)}, bf16[1,32,2048]{2,1,0:T(8,128)(2,1)S(1)}, u32[]{:S(2)}, u32[]{:S(2)}) collective-permute-start(bf16[1,32,2048]{2,1,0:T(8,128)(2,1)S(1)} %get-tuple-element.12), channel_id=1, source_target_pairs={{0,10},{1,11},{2,8},{3,9},{4,14},{5,15},{6,12},{7,13},{8,2},{9,3},... | collective-permute-start | bytes 393224 | tf_op jit(solution)/shard_map/ppermute | solution.py:28
  39.6 28.4 %collective-permute-start.10 = (bf16[1,32,2048]{2,1,0:T(8,128)(2,1)S(1)}, bf16[1,32,2048]{2,1,0:T(8,128)(2,1)S(1)}, u32[]{:S(2)}, u32[]{:S(2)}) collective-permute-start(bf16[1,32,2048]{2,1,0:T(8,128)(2,1)S(1)} %get-tuple-element.11), channel_id=1, source_target_pairs={{0,11},{1,10},{2,9},{3,8},{4,15},{5,14},{6,13},{7,12},{8,3},{9,2},... | collective-permute-start | bytes 393224 | tf_op jit(solution)/shard_map/ppermute | solution.py:28
  46.9 26.9 %collective-permute-start.11 = (bf16[1,32,2048]{2,1,0:T(8,128)(2,1)S(1)}, bf16[1,32,2048]{2,1,0:T(8,128)(2,1)S(1)}, u32[]{:S(2)}, u32[]{:S(2)}) collective-permute-start(bf16[1,32,2048]{2,1,0:T(8,128)(2,1)S(1)} %get-tuple-element.10), channel_id=1, source_target_pairs={{0,12},{1,13},{2,14},{3,15},{4,8},{5,9},{6,10},{7,11},{8,4},{9,5},... | collective-permute-start | bytes 393224 | tf_op jit(solution)/shard_map/ppermute | solution.py:28
  48.3 28.4 %collective-permute-start.12 = (bf16[1,32,2048]{2,1,0:T(8,128)(2,1)S(1)}, bf16[1,32,2048]{2,1,0:T(8,128)(2,1)S(1)}, u32[]{:S(2)}, u32[]{:S(2)}) collective-permute-start(bf16[1,32,2048]{2,1,0:T(8,128)(2,1)S(1)} %get-tuple-element.9), channel_id=1, source_target_pairs={{0,13},{1,12},{2,15},{3,14},{4,9},{5,8},{6,11},{7,10},{8,5},{9,4},... | collective-permute-start | bytes 393224 | tf_op jit(solution)/shard_map/ppermute | solution.py:28
  59.7 19.8 %collective-permute-start.13 = (bf16[1,32,2048]{2,1,0:T(8,128)(2,1)S(1)}, bf16[1,32,2048]{2,1,0:T(8,128)(2,1)S(1)}, u32[]{:S(2)}, u32[]{:S(2)}) collective-permute-start(bf16[1,32,2048]{2,1,0:T(8,128)(2,1)S(1)} %get-tuple-element.8), channel_id=1, source_target_pairs={{0,14},{1,15},{2,12},{3,13},{4,10},{5,11},{6,8},{7,9},{8,6},{9,7},... | collective-permute-start | bytes 393224 | tf_op jit(solution)/shard_map/ppermute | solution.py:28
  62.5 19.8 %collective-permute-start.14 = (bf16[1,32,2048]{2,1,0:T(8,128)(2,1)S(1)}, bf16[1,32,2048]{2,1,0:T(8,128)(2,1)S(1)}, u32[]{:S(2)}, u32[]{:S(2)}) collective-permute-start(bf16[1,32,2048]{2,1,0:T(8,128)(2,1)S(1)} %get-tuple-element.7), channel_id=1, source_target_pairs={{0,15},{1,14},{2,13},{3,12},{4,11},{5,10},{6,9},{7,8},{8,7},{9,6},... | collective-permute-start | bytes 393224 | tf_op jit(solution)/shard_map/ppermute | solution.py:28
  82.3 1.8 %copy-start.8 = (bf16[1,384,2048]{2,1,0:T(8,128)(2,1)S(1)}, bf16[1,384,2048]{2,1,0:T(8,128)(2,1)}, u32[]{:S(2)}) copy-start(bf16[1,384,2048]{2,1,0:T(8,128)(2,1)} %param.19) | copy-start | bytes 4718596
  86.7 6.4 %copy-start.7 = (pred[64,8]{0,1:T(8,128)(4,1)S(1)}, pred[64,8]{0,1:T(8,128)(4,1)}, u32[]{:S(2)}) copy-start(pred[64,8]{0,1:T(8,128)(4,1)} %get-tuple-element.5) | copy-start | bytes 1540
  86.7 6.5 %copy-start.4 = (f32[1,64,8]{1,2,0:T(8,128)S(1)}, f32[1,64,8]{1,2,0:T(8,128)}, u32[]{:S(2)}) copy-start(f32[1,64,8]{1,2,0:T(8,128)} %param.16) | copy-start | bytes 6148
  86.7 53.8 %all-to-all-start = ((bf16[16,32,2048]{2,1,0:T(8,128)(2,1)}), bf16[16,32,2048]{2,1,0:T(8,128)(2,1)}, u32[]{:S(2)}, u32[]{:S(2)}) async-start(bf16[16,32,2048]{2,1,0:T(8,128)(2,1)} %bitcast.88), calls=%async_computation | async-start | bytes 4194304 | tf_op jit(solution)/shard_map/all_to_all | solution.py:155
  147.6 3.9 %copy-start.2 = (bf16[1,64,2048]{2,1,0:T(8,128)(2,1)S(1)}, bf16[1,64,2048]{2,1,0:T(8,128)(2,1)}, u32[]{:S(2)}) copy-start(bf16[1,64,2048]{2,1,0:T(8,128)(2,1)} %param.10) | copy-start | bytes 786436
